TPU v7x, 32 devices: a whole 2x2x4 slice. The times are simulated.
32 devices in a mesh: azi: 8 (over z, y), wall: 4 (over x, core).
Axes of the slice: x: 2, y: 2, z: 4, core: 2. Of those that a mesh axis runs over, the one named last changes fastest.
Arguments:
- state: float32 [5, 32, 128, 128], P(None, 'azi', 'wall'), may hold values from -6 to 6
- flux_azi: float32 [5, 5], replicated, may hold values from -2.5 to 2.5
- flux_wall: float32 [5, 5], replicated, may hold values from -2.5 to 2.5
- to_wall: float32 [5, 5], replicated, may hold values from -2.5 to 2.5
- mix_char: float32 [5, 5], replicated, may hold values from -2.5 to 2.5
- from_azi: float32 [5, 5], replicated, may hold values from -2.5 to 2.5
- speed_azi: float32 [5, 32], P(None, 'azi'), may hold values from -1 to 1
- speed_wall: float32 [5, 128], P(None, 'wall'), may hold values from -1 to 1
- visc_azi: float32 [5], replicated, may hold values from 2048 to 16384
- visc_wall: float32 [5], replicated, may hold values from 2048 to 16384
Outputs:
- increment: float32 [5, 32, 128, 128], P(None, 'azi', 'wall')
All inputs are finite; a program needn't handle non-finite values.
Results may differ from a plain program's by a relative error of at most 0.0009.
Values sent between devices are 32-bit elements; how exact they have to be, the bound alone decides.
A program may use at most 128 MiB of HBM per device.

v0:
```python
import functools

import jax
import jax.numpy as jnp
from jax import lax
from jax.experimental import pallas as pl
from jax.experimental.pallas import tpu as pltpu
from jax.sharding import PartitionSpec as P

time_step = 4096.0
smooth_explicit = 0.02
smooth_implicit = 0.04
highest = lax.Precision.HIGHEST


def padded(value, sides, width, wrap):
    for axis, dim in sides:
        size, length = (lax.axis_size(axis), value.shape[dim])
        up = [(i, (i + 1) % size) for i in range(size if wrap else size - 1)]
        down = [(j, i) for i, j in up]
        last = lax.slice_in_dim(value, length - width, length, axis=dim)
        initial = lax.slice_in_dim(value, 0, width, axis=dim)
        before = lax.ppermute(last, axis, up)
        after = lax.ppermute(initial, axis, down)
        value = jnp.concatenate([before, value, after], axis=dim)
    return value


def from_behind(value, axis, by):
    size = lax.axis_size(axis)
    pairs = [(i, i + by) for i in range(size) if 0 <= i + by < size]
    return lax.ppermute(value, axis, pairs)


def from_behind_2(block, axis, distance):
    devices = range(lax.axis_size(axis))
    route = [((i - distance) % len(devices), i) for i in devices]
    return lax.ppermute(block, axis, route)


def mixing(matrix, field):
    return jnp.einsum("ab,bjkl->ajkl", matrix, field, precision=highest)


def residual(padded_azi, padded_wall, flux_azi, flux_wall):
    azi_flux = mixing(flux_azi, padded_azi[:, 1:-1])
    wall_flux = mixing(flux_wall, padded_wall[:, :, 1:-1])
    central = 0.5 * (azi_flux[:, 2:] - azi_flux[:, :-2]) + 0.5 * (
        wall_flux[:, :, 2:] - wall_flux[:, :, :-2]
    )
    fourth = (
        padded_azi[:, 4:]
        - 4.0 * padded_azi[:, 3:-1]
        + 6.0 * padded_azi[:, 2:-2]
        - 4.0 * padded_azi[:, 1:-3]
        + padded_azi[:, :-4]
    )
    fourth = (
        fourth
        + padded_wall[:, :, 4:]
        - 4.0 * padded_wall[:, :, 3:-1]
        + 6.0 * padded_wall[:, :, 2:-2]
        - 4.0 * padded_wall[:, :, 1:-3]
        + padded_wall[:, :, :-4]
    )
    return -time_step * (central + smooth_explicit * fourth)


def coefficients(speed, visc):
    viscous = visc[:, None]
    below = -0.5 * time_step * speed - viscous - 4.0 * smooth_implicit
    above = 0.5 * time_step * speed - viscous - 4.0 * smooth_implicit
    centre = 1.0 + 2.0 * viscous + 6.0 * smooth_implicit
    return (below, above, centre)


def invert(matrices):
    extent = matrices.shape[-1]
    last_axis = matrices.ndim - 1
    identity = jnp.broadcast_to(jnp.eye(extent, dtype=matrices.dtype), matrices.shape)
    marks = lax.broadcasted_iota(jnp.int32, (extent, 1), 0)

    def eliminate(turn, running):
        working, inverse = running
        pivot_row = lax.dynamic_index_in_dim(working, turn, last_axis - 1, keepdims=False)
        inverse_row = lax.dynamic_index_in_dim(inverse, turn, last_axis - 1, keepdims=False)
        column = lax.dynamic_index_in_dim(working, turn, last_axis, keepdims=True)
        pivot = lax.dynamic_index_in_dim(pivot_row, turn, last_axis - 1, keepdims=True)
        pivot_row = pivot_row / pivot
        inverse_row = inverse_row / pivot
        working = working - column * pivot_row[..., None, :]
        inverse = inverse - column * inverse_row[..., None, :]
        on_row = marks == turn
        working = jnp.where(on_row, pivot_row[..., None, :], working)
        inverse = jnp.where(on_row, inverse_row[..., None, :], inverse)
        return (working, inverse)

    return lax.fori_loop(0, extent, eliminate, (matrices, identity))[1]


def two_by_two(first, second, third, fourth):
    return jnp.stack([jnp.stack([first, second], -1), jnp.stack([third, fourth], -1)], -2)


def invert_two(blocks):
    first = blocks[..., 0, 0]
    second = blocks[..., 0, 1]
    third = blocks[..., 1, 0]
    fourth = blocks[..., 1, 1]
    determinant = first * fourth - second * third
    return two_by_two(
        fourth / determinant, -second / determinant, -third / determinant, first / determinant
    )


def block_product(first, second):
    return jnp.einsum("cmab,cmbd->cmad", first, second, precision=highest)


def block_apply(blocks, field):
    return jnp.einsum("cmab,cmbkl->cmakl", blocks, field, precision=highest)


def apply_four(matrix, field):
    return jnp.einsum("cqr,cjrl->cjql", matrix, field, precision=highest)


def product_four(first, second):
    return jnp.einsum("cab,cbd->cad", first, second, precision=highest)


def cyclic_levels(speeds, visc):
    below, above, centre = coefficients(speeds, visc)
    below_even = below[:, 0::2]
    below_odd = below[:, 1::2]
    above_even = above[:, 0::2]
    above_odd = above[:, 1::2]
    edge_value = jnp.full_like(below_even, smooth_implicit)
    nought = jnp.zeros_like(below_even)
    middle_diag = jnp.broadcast_to(centre, below_even.shape)
    behind_block = two_by_two(edge_value, below_even, nought, edge_value)
    middle = two_by_two(middle_diag, above_even, below_odd, middle_diag)
    ahead_block = two_by_two(edge_value, nought, above_odd, edge_value)
    blocks = below_even.shape[1]
    stride = 1
    levels = []
    while stride < blocks:
        weight_before = -block_product(behind_block, invert_two(jnp.roll(middle, stride, 1)))
        weight_after = -block_product(ahead_block, invert_two(jnp.roll(middle, -stride, 1)))
        middle = (
            middle
            + block_product(weight_before, jnp.roll(ahead_block, stride, 1))
            + block_product(weight_after, jnp.roll(behind_block, -stride, 1))
        )
        behind_block = block_product(weight_before, jnp.roll(behind_block, stride, 1))
        ahead_block = block_product(weight_after, jnp.roll(ahead_block, -stride, 1))
        levels.append((stride, weight_before, weight_after))
        stride = stride * 2
    return (levels, invert_two(behind_block + middle + ahead_block))


def per_device(
    state,
    flux_azi,
    flux_wall,
    to_wall,
    mix_char,
    from_azi,
    speed_azi,
    speed_wall,
    visc_azi,
    visc_wall,
):
    padded_azi = padded(state, (("azi", 1),), 2, True)
    padded_wall = padded(state, (("wall", 2),), 2, False)
    explicit = residual(padded_azi, padded_wall, flux_azi, flux_wall)
    char_wall = mixing(to_wall, explicit)
    variables = state.shape[0]
    cycle_cells = state.shape[1]
    wall_depth = state.shape[2]
    span_cells = state.shape[3]
    below, above, centre = coefficients(speed_wall, visc_wall)

    def shifted(offset):
        return jnp.eye(wall_depth, k=offset, dtype=jnp.float32)

    wall_band = (
        centre[:, :, None] * shifted(0)
        + below[:, :, None] * shifted(-1)
        + above[:, :, None] * shifted(1)
        + smooth_implicit * (shifted(2) + shifted(-2))
    )
    local_inverse = invert(wall_band)
    solved = jnp.einsum("ckm,cjml->cjkl", local_inverse, char_wall, precision=highest)
    edge_value = jnp.full_like(below[:, 0], smooth_implicit)
    nought = jnp.zeros_like(edge_value)
    spike_low = jnp.einsum(
        "cka,cab->ckb",
        local_inverse[:, :, 0:2],
        two_by_two(edge_value, below[:, 0], nought, edge_value),
        precision=highest,
    )
    spike_high = jnp.einsum(
        "cka,cab->ckb",
        local_inverse[:, :, wall_depth - 2 :],
        two_by_two(edge_value, nought, above[:, wall_depth - 1], edge_value),
        precision=highest,
    )
    padding = jnp.zeros((variables, 4, 2), jnp.float32)
    ends_low = jnp.concatenate([spike_low[:, 0:2], spike_low[:, wall_depth - 2 :]], 1)
    ends_high = jnp.concatenate([spike_high[:, 0:2], spike_high[:, wall_depth - 2 :]], 1)
    coupling_prev = jnp.concatenate([padding, ends_low], 2)
    coupling_next = jnp.concatenate([ends_high, padding], 2)
    interface = jnp.concatenate([solved[:, :, 0:2], solved[:, :, wall_depth - 2 :]], 2)
    wall_place = lax.axis_index("wall")
    wall_count = lax.axis_size("wall")
    every_prev, every_next = (
        lax.all_gather(coupling_prev, "wall", axis=1, tiled=True),
        lax.all_gather(coupling_next, "wall", axis=1, tiled=True),
    )
    carried = jnp.zeros((variables, 4, 4), jnp.float32)
    identity = jnp.broadcast_to(jnp.eye(4, dtype=jnp.float32), (variables, 4, 4))
    inverses = []
    forwards = []
    for member in range(wall_count):
        pivot_block = identity - product_four(every_prev[:, 4 * member : 4 * member + 4], carried)
        pivot_inverse = invert(pivot_block)
        carried = product_four(pivot_inverse, every_next[:, 4 * member : 4 * member + 4])
        inverses.append(pivot_inverse)
        forwards.append(carried)
    own_inverse = lax.dynamic_index_in_dim(jnp.stack(inverses), wall_place, 0, keepdims=False)
    own_forward = lax.dynamic_index_in_dim(jnp.stack(forwards), wall_place, 0, keepdims=False)
    partial_values = jnp.zeros_like(interface)
    for turn in range(wall_count):
        arrived = from_behind(partial_values, "wall", 1)
        fresh = apply_four(own_inverse, interface - apply_four(coupling_prev, arrived))
        partial_values = jnp.where(wall_place == turn, fresh, partial_values)
    end_values = jnp.zeros_like(interface)
    ahead = jnp.zeros((variables, cycle_cells, 2, span_cells), jnp.float32)
    for turn in reversed(range(wall_count)):
        arrived = from_behind(end_values, "wall", -1)
        fresh = partial_values - apply_four(own_forward, arrived)
        end_values = jnp.where(wall_place == turn, fresh, end_values)
        ahead = jnp.where(wall_place == turn, arrived[:, :, 0:2], ahead)
    behind = from_behind(end_values, "wall", 1)[:, :, 2:4]
    wall_result = (
        solved
        - jnp.einsum("cka,cjal->cjkl", spike_low, behind, precision=highest)
        - jnp.einsum("cka,cjal->cjkl", spike_high, ahead, precision=highest)
    )
    cycle_input = mixing(mix_char, wall_result)
    speeds = lax.all_gather(speed_azi, "azi", axis=1, tiled=True)
    levels, closing = cyclic_levels(speeds, visc_azi)
    half_cells = cycle_cells // 2
    cycle_place = lax.axis_index("azi")

    def own_rows(blocks):
        return lax.dynamic_slice_in_dim(blocks, cycle_place * half_cells, half_cells, 1)

    right_side = cycle_input.reshape(variables, half_cells, 2, wall_depth, span_cells)
    for stride, weight_before, weight_after in levels:
        device_hop = max(1, stride // half_cells)
        reach = min(stride, half_cells)
        from_before = from_behind_2(right_side[:, half_cells - reach :], "azi", device_hop)
        from_after = from_behind_2(right_side[:, :reach], "azi", -device_hop)
        rows_minus = jnp.concatenate([from_before, right_side[:, : half_cells - reach]], 1)
        rows_plus = jnp.concatenate([right_side[:, reach:], from_after], 1)
        right_side = (
            right_side
            + block_apply(own_rows(weight_before), rows_minus)
            + block_apply(own_rows(weight_after), rows_plus)
        )
    cycle_result = block_apply(own_rows(closing), right_side).reshape(
        variables, cycle_cells, wall_depth, span_cells
    )
    return mixing(from_azi, cycle_result)


MESH = pl.DeviceIdType.MESH


def band(speed, visc):
    below = -0.5 * time_step * speed - visc - 4.0 * smooth_implicit
    above = 0.5 * time_step * speed - visc - 4.0 * smooth_implicit
    centre = 1.0 + 2.0 * visc + 6.0 * smooth_implicit
    both = below + above
    part = both - below
    lost = (below - (both - part)) + (above - part)
    total = (centre + both) + lost + 2.0 * smooth_implicit
    return below, above, total


def mix(matrix_ref, fields):
    result = []
    for a in range(len(fields)):
        value = matrix_ref[a, 0] * fields[0]
        for b in range(1, len(fields)):
            value = value + matrix_ref[a, b] * fields[b]
        result.append(value)
    return result


def wall_inverse(speeds_ref, visc, wide_ref, alpha_ref, beta_ref, inverse_ref):
    walls, variables, part = speeds_ref.shape
    cells = walls * part
    lanes = wide_ref.shape[-1]
    for w in range(walls):
        block = speeds_ref[w]
        for k in range(part):
            wide_ref[w * part + k] = jnp.broadcast_to(block[:, k : k + 1], (variables, lanes))
    lane = lax.broadcasted_iota(jnp.int32, (variables, lanes), 1)
    both = lane + lax.broadcasted_iota(jnp.int32, (variables, lanes), 0)
    zero = jnp.where(both < 0, 1.0, 0.0)
    one = jnp.where(both < 0, 0.0, 1.0)

    def forward(k, carry):
        alpha1, beta1, gamma1, sum1, alpha2, beta2, gamma2, sum2 = carry
        below, above, total = band(wide_ref[k], visc)
        lower = below - smooth_implicit * alpha2
        upper = above - lower * beta1
        total = (total - smooth_implicit * sum2) - lower * sum1
        pivot = total - upper - smooth_implicit
        inverse = 1.0 / pivot
        right = jnp.where(lane == k, 1.0, 0.0) - smooth_implicit * gamma2 - lower * gamma1
        alpha = upper * inverse
        beta = smooth_implicit * inverse
        gamma = right * inverse
        alpha_ref[k] = alpha
        beta_ref[k] = beta
        inverse_ref[pl.ds(pl.multiple_of(k * 8, 8), variables), :] = gamma
        return (alpha, beta, gamma, total * inverse, alpha1, beta1, gamma1, sum1)

    lax.fori_loop(0, cells, forward, (zero, zero, zero, one, zero, zero, zero, one), unroll=2)

    def backward(turn, carry):
        x1, x2 = carry
        k = cells - 1 - turn
        rows = pl.ds(pl.multiple_of(k * 8, 8), variables)
        x = (inverse_ref[rows, :] - beta_ref[k] * x2) - alpha_ref[k] * x1
        inverse_ref[rows, :] = x
        return (x, x1)

    lax.fori_loop(0, cells, backward, (zero, zero), unroll=2)


def cycle_inverse(speeds_ref, visc, span, inverse_ref):
    azis, variables, part = speeds_ref.shape
    cells = azis * part
    lanes = inverse_ref.shape[-1]
    lane = lax.broadcasted_iota(jnp.int32, (variables, lanes), 1)
    own_cell = (lane % (azis * span)) // span * part + lane // (azis * span)
    zero = jnp.zeros((variables, lanes), jnp.float32)
    one = jnp.ones((variables, lanes), jnp.float32)

    def row(j):
        speed = jnp.broadcast_to(
            speeds_ref[j // part][:, j % part : j % part + 1], (variables, lanes)
        )
        return band(speed, visc) + (jnp.where(own_cell == j, 1.0, 0.0),)

    one_back = (zero, zero, zero, zero, -one, zero)
    two_back = (zero, zero, zero, -one, zero, zero)
    rows = []
    for j in range(cells - 2):
        below, above, total, right = row(j)
        lower = below - smooth_implicit * two_back[0]
        upper = above - lower * one_back[1]
        first = -smooth_implicit * two_back[3] - lower * one_back[3]
        second = -smooth_implicit * two_back[4] - lower * one_back[4]
        total = (total - smooth_implicit * two_back[5]) - lower * one_back[5]
        pivot = total - upper - smooth_implicit - first - second
        inverse = 1.0 / pivot
        right = right - smooth_implicit * two_back[2] - lower * one_back[2]
        two_back = one_back
        one_back = (
            upper * inverse,
            smooth_implicit * inverse,
            right * inverse,
            first * inverse,
            second * inverse,
            total * inverse,
        )
        rows.append(one_back)
    after = (zero, zero, -one, zero)
    later = (zero, -one, zero, zero)
    known = [None] * (cells - 2)
    ahead1, ahead2 = (zero, -one, zero, zero), (zero, zero, -one, zero)
    for j in reversed(range(cells - 2)):
        alpha, beta, gamma, first, second, total = rows[j]
        start = (gamma, first, second, total)
        now = tuple(
            (s - beta * far) - alpha * near for s, near, far in zip(start, ahead1, ahead2)
        )
        known[j] = now
        ahead2, ahead1 = ahead1, now
    below, above, total0, right0 = row(cells - 2)
    third, fourth = known[cells - 4], known[cells - 3]
    a01 = above - smooth_implicit * third[2] - below * fourth[2] - smooth_implicit * known[0][2]
    total0 = total0 - smooth_implicit * third[3] - below * fourth[3] - smooth_implicit * known[0][3]
    right0 = right0 - smooth_implicit * third[0] - below * fourth[0] - smooth_implicit * known[0][0]
    below, above, total1, right1 = row(cells - 1)
    a10 = below - smooth_implicit * fourth[1] - above * known[0][1] - smooth_implicit * known[1][1]
    total1 = total1 - smooth_implicit * fourth[3] - above * known[0][3] - smooth_implicit * known[1][3]
    right1 = right1 - smooth_implicit * fourth[0] - above * known[0][0] - smooth_implicit * known[1][0]
    scale = 1.0 / (total0 * total1 - total0 * a10 - total1 * a01)
    value0 = ((total1 - a10) * right0 - a01 * right1) * scale
    value1 = ((total0 - a01) * right1 - a10 * right0) * scale
    values = [k[0] - k[1] * value0 - k[2] * value1 for k in known] + [value0, value1]
    place = lane % span
    for j in range(cells):
        base = (j % part) * azis * span + (j // part) * span
        for l in range(span):
            inverse_ref[pl.ds((base + l) * 8, variables), :] = jnp.where(place == l, values[j], 0.0)


def step_kernel(
    azis,
    walls,
    state_ref,
    speed_azi_ref,
    speed_wall_ref,
    flux_azi_ref,
    flux_wall_ref,
    to_wall_ref,
    mix_char_ref,
    from_azi_ref,
    visc_azi_ref,
    visc_wall_ref,
    out_ref,
    send1,
    recv1,
    send2,
    recv2,
    all_azi,
    all_wall,
    wide,
    alphas,
    betas,
    wall_inv,
    cycle_inv,
    rows_ref,
    blocks,
    fields,
    send1_sem,
    recv1_sem,
    send2_sem,
    recv2_sem,
    azi_send,
    azi_recv,
    wall_send,
    wall_recv,
    own_sem,
):
    variables, part_j, part_k, span_all = state_ref.shape
    count = azis * walls
    span = span_all // count
    lanes = part_j * part_k
    group = azis * span
    wall_cells = walls * part_k
    me_azi = lax.axis_index("azi")
    me_wall = lax.axis_index("wall")
    me = me_azi * walls + me_wall

    barrier = pltpu.get_barrier_semaphore()

    def other(turn):
        target = lax.rem(me + turn, count)
        return target, target // walls, lax.rem(target, walls)

    def greet(turn, _):
        target, azi, wall = other(turn)
        pl.semaphore_signal(barrier, inc=1, device_id=(azi, wall), device_id_type=MESH)
        return 0

    lax.fori_loop(1, count, greet, 0)

    for c in range(variables):
        turned = state_ref[c].reshape(lanes, span_all).T
        for t in range(count):
            send1[c, t] = turned[t * span : (t + 1) * span]

    pl.semaphore_wait(barrier, count - 1)

    def azi_copy(turn):
        azi = lax.rem(me_azi + turn, azis)
        return pltpu.make_async_remote_copy(
            src_ref=speed_azi_ref,
            dst_ref=all_azi.at[me_azi],
            send_sem=azi_send.at[turn],
            recv_sem=azi_recv.at[me_azi],
            device_id=(azi, me_wall),
            device_id_type=MESH,
        )

    def wall_copy(turn):
        wall = lax.rem(me_wall + turn, walls)
        return pltpu.make_async_remote_copy(
            src_ref=speed_wall_ref,
            dst_ref=all_wall.at[me_wall],
            send_sem=wall_send.at[turn],
            recv_sem=wall_recv.at[me_wall],
            device_id=(me_azi, wall),
            device_id_type=MESH,
        )

    def out_copy(turn):
        target, azi, wall = other(turn)
        return pltpu.make_async_remote_copy(
            src_ref=send1.at[:, target],
            dst_ref=recv1.at[me_wall, :, me_azi],
            send_sem=send1_sem.at[turn],
            recv_sem=recv1_sem.at[me],
            device_id=(azi, wall),
            device_id_type=MESH,
        )

    def back_copy(turn):
        target, azi, wall = other(turn)
        return pltpu.make_async_remote_copy(
            src_ref=send2.at[wall, :, azi],
            dst_ref=recv2.at[:, me],
            send_sem=send2_sem.at[turn],
            recv_sem=recv2_sem.at[me],
            device_id=(azi, wall),
            device_id_type=MESH,
        )

    def start_all(make, stop):
        def one(turn, _):
            make(turn).start()
            return 0

        lax.fori_loop(1, stop, one, 0)

    def sent_all(make, stop):
        def one(turn, _):
            make(turn).wait_send()
            return 0

        lax.fori_loop(1, stop, one, 0)

    start_all(wall_copy, walls)
    start_all(azi_copy, azis)
    start_all(out_copy, count)
    own = pltpu.make_async_copy(send1.at[:, me], recv1.at[me_wall, :, me_azi], own_sem.at[0])
    own.start()
    own_azi = pltpu.make_async_copy(speed_azi_ref, all_azi.at[me_azi], own_sem.at[1])
    own_azi.start()
    own_wall = pltpu.make_async_copy(speed_wall_ref, all_wall.at[me_wall], own_sem.at[2])
    own_wall.start()

    def arrived(ref_of, sems, me_index, stop):
        def one(turn, _):
            source = lax.rem(me_index + turn, stop)
            ref = ref_of(source)
            pltpu.make_async_copy(ref, ref, sems.at[source]).wait()
            return 0

        lax.fori_loop(1, stop, one, 0)

    def viscosity(ref):
        index = lax.broadcasted_iota(jnp.int32, (variables, lanes), 0)
        value = jnp.full((variables, lanes), ref[0], jnp.float32)
        for c in range(1, variables):
            value = jnp.where(index == c, ref[c], value)
        return value

    own_wall.wait()
    arrived(lambda w: all_wall.at[w], wall_recv, me_wall, walls)
    wall_inverse(all_wall, viscosity(visc_wall_ref), wide, alphas, betas, wall_inv)
    own_azi.wait()
    arrived(lambda a: all_azi.at[a], azi_recv, me_azi, azis)
    cycle_inverse(all_azi, viscosity(visc_azi_ref), span, cycle_inv)

    own.wait()
    arrived(
        lambda s: recv1.at[lax.rem(s, walls), :, s // walls], recv1_sem, me, count
    )
    lane = lax.broadcasted_iota(jnp.int32, (group, lanes), 1)
    piece = lane // part_k
    for c in range(variables):
        for w in range(walls):
            for a in range(azis):
                rows_ref[c, w, pl.ds(a * span, span), :] = recv1[w, c, a]
    for c in range(variables):
        parts = [rows_ref[c, w] for w in range(walls)]
        for m in range(part_j):
            value = parts[m % walls]
            for w in range(walls):
                moved = parts[w]
                if w != m:
                    moved = pltpu.roll(moved, ((w - m) * part_k) % lanes, 1)
                value = jnp.where(piece == w, moved, value) if w else moved
            blocks[c, m] = value

    def cell(c, m):
        value = blocks[c, m % part_j]
        turns = m // part_j
        return pltpu.roll(value, (-turns * span) % group, 0) if turns else value

    def along(value, by):
        moved = pltpu.roll(value, (-by) % wall_cells, 1)
        keep = lane < wall_cells - by if by > 0 else lane >= -by
        return jnp.where(keep, moved, 0.0)

    for m in range(part_j):
        central_j, central_k, fourth = [], [], []
        for c in range(variables):
            here = cell(c, m)
            up1, up2 = cell(c, m + 1), cell(c, m + 2)
            down1, down2 = cell(c, m - 1), cell(c, m - 2)
            right1, right2 = along(here, 1), along(here, 2)
            left1, left2 = along(here, -1), along(here, -2)
            central_j.append(0.5 * (up1 - down1))
            central_k.append(0.5 * (right1 - left1))
            fourth.append(
                (up2 + down2) + (right2 + left2) - 4.0 * ((up1 + down1) + (right1 + left1)) + 12.0 * here
            )
        flux_j = mix(flux_azi_ref, central_j)
        flux_k = mix(flux_wall_ref, central_k)
        explicit = [
            -time_step * (flux_j[c] + flux_k[c] + smooth_explicit * fourth[c])
            for c in range(variables)
        ]
        turned = mix(to_wall_ref, explicit)
        for c in range(variables):
            fields[c, pl.ds(m * group, group), :] = turned[c]

    for c in range(variables):
        inverse = wall_inv[pl.ds(c, wall_cells, stride=8), :]
        fields[c] = lax.dot_general(
            fields[c],
            inverse,
            (((1,), (1,)), ((), ())),
            precision=highest,
            preferred_element_type=jnp.float32,
        )
    for m in range(part_j):
        rows = pl.ds(m * group, group)
        mixed = mix(mix_char_ref, [fields[c, rows, :] for c in range(variables)])
        for c in range(variables):
            fields[c, rows, :] = mixed[c]
    for c in range(variables):
        inverse = cycle_inv[pl.ds(c, part_j * group, stride=8), :]
        fields[c] = jnp.dot(
            inverse, fields[c], precision=highest, preferred_element_type=jnp.float32
        )
    for m in range(part_j):
        rows = pl.ds(m * group, group)
        mixed = mix(from_azi_ref, [fields[c, rows, :] for c in range(variables)])
        for c in range(variables):
            blocks[c, m] = mixed[c]
    for c in range(variables):
        parts = [blocks[c, m] for m in range(part_j)]
        for w in range(walls):
            value = None
            for m in range(part_j):
                moved = parts[m]
                if w != m:
                    moved = pltpu.roll(moved, ((m - w) * part_k) % lanes, 1)
                value = jnp.where(piece == m, moved, value) if m else moved
            for a in range(azis):
                send2[w, c, a] = value[a * span : (a + 1) * span]

    start_all(back_copy, count)
    own_back = pltpu.make_async_copy(send2.at[me_wall, :, me_azi], recv2.at[:, me], own_sem.at[0])
    own_back.start()
    sent_all(wall_copy, walls)
    sent_all(azi_copy, azis)
    sent_all(out_copy, count)
    own_back.wait()
    arrived(lambda s: recv2.at[:, s], recv2_sem, me, count)
    for c in range(variables):
        for s in range(count):
            fields[c, pl.ds(s * span, span), :] = recv2[c, s]
    for c in range(variables):
        out_ref[c] = fields[c].T.reshape(part_j, part_k, span_all)
    sent_all(back_copy, count)


def per_device_whole_lines(
    state,
    flux_azi,
    flux_wall,
    to_wall,
    mix_char,
    from_azi,
    speed_azi,
    speed_wall,
    visc_azi,
    visc_wall,
):
    azis, walls = lax.axis_size("azi"), lax.axis_size("wall")
    count = azis * walls
    variables, part_j, part_k, span_all = state.shape
    span = span_all // count
    lanes = part_j * part_k
    wall_cells = walls * part_k
    vmem = pl.BlockSpec(memory_space=pltpu.VMEM)
    smem = pl.BlockSpec(memory_space=pltpu.SMEM)
    f32 = jnp.float32
    dma = pltpu.SemaphoreType.DMA
    return pl.pallas_call(
        functools.partial(step_kernel, azis, walls),
        out_shape=jax.ShapeDtypeStruct(state.shape, f32),
        in_specs=[vmem] * 3 + [smem] * 7,
        out_specs=vmem,
        scratch_shapes=[
            pltpu.VMEM((variables, count, span, lanes), f32),
            pltpu.VMEM((walls, variables, azis, span, lanes), f32),
            pltpu.VMEM((walls, variables, azis, span, lanes), f32),
            pltpu.VMEM((variables, count, span, lanes), f32),
            pltpu.VMEM((azis,) + speed_azi.shape, f32),
            pltpu.VMEM((walls,) + speed_wall.shape, f32),
            pltpu.VMEM((wall_cells, variables, lanes), f32),
            pltpu.VMEM((wall_cells, variables, lanes), f32),
            pltpu.VMEM((wall_cells, variables, lanes), f32),
            pltpu.VMEM((wall_cells * 8, lanes), f32),
            pltpu.VMEM((part_j * azis * span * 8, lanes), f32),
            pltpu.VMEM((variables, walls, azis * span, lanes), f32),
            pltpu.VMEM((variables, part_j, azis * span, lanes), f32),
            pltpu.VMEM((variables, span_all, lanes), f32),
            dma((count,)),
            dma((count,)),
            dma((count,)),
            dma((count,)),
            dma((azis,)),
            dma((azis,)),
            dma((walls,)),
            dma((walls,)),
            dma((3,)),
        ],
        compiler_params=pltpu.CompilerParams(collective_id=0, has_side_effects=True),
    )(
        state,
        speed_azi,
        speed_wall,
        flux_azi,
        flux_wall,
        to_wall,
        mix_char,
        from_azi,
        visc_azi,
        visc_wall,
    )


def whole_lines_fit(mesh, variables, part_j, part_k, span_all):
    azis, walls = mesh.shape["azi"], mesh.shape["wall"]
    count = azis * walls
    lanes = part_j * part_k
    return (
        span_all % count == 0
        and lanes == 128
        and span_all == lanes
        and walls * part_k == lanes
        and walls == part_j
        and azis * (span_all // count) * part_j == lanes
        and (azis * (span_all // count)) % 8 == 0
        and azis * part_j >= 8
        and variables <= 8
    )


def solution(mesh):
    in_specs = (
        P(None, "azi", "wall", None),
        P(),
        P(),
        P(),
        P(),
        P(),
        P(None, "azi"),
        P(None, "wall"),
        P(),
        P(),
    )
    out_specs = P(None, "azi", "wall", None)

    def chosen(state, *rest):
        if whole_lines_fit(mesh, *state.shape):
            return per_device_whole_lines(state, *rest)
        return per_device(state, *rest)

    return jax.shard_map(
        chosen, mesh=mesh, in_specs=in_specs, out_specs=out_specs, check_vma=False
    )
```

profile of v0, /device:TPU:25, one launch (start us, length us, event | category | flops | bytes accessed | tf_op | source)
XLA Modules:
  0.0 32.5 jit_solution(17046918636335613690)
XLA Ops:
  0.0 1.4 %copy.11.speed_azi_ref = f32[5,4]{1,0:T(8,128)} copy(f32[5,4]{0,1:T(4,128)} %param.16) | data formatting | bytes 160 | tf_op args[6]
  1.4 29.4 %shard_map.100 = f32[5,4,32,128]{3,2,1,0:T(8,128)} custom-call(f32[5,4,32,128]{3,2,1,0:T(8,128)} %state_ref.1, f32[5,4]{1,0:T(8,128)} %copy.11.speed_azi_ref, f32[5,32]{1,0:T(8,128)} %speed_wall_ref.1, f32[5,5]{1,0:T(8,128)} %flux_azi_ref.1, f32[5,5]{1,0:T(8,128)} %flux_wall_ref.1, f32[5,5]{1,0:T(8,128)} %to_wall_ref.1, f32[5,5]{1,0:T(8,128)} %mix_char_ref.1, ...), custom_call_target="tpu_custom_call" | custom-call | tf_op jit(solution)/shard_map/pallas_call | solution.py:703
  30.7 1.7 %copy.13 = f32[5,4,32,128]{3,2,1,0:T(8,128)} copy(f32[5,4,32,128]{3,2,1,0:T(8,128)} %shard_map.100) | data formatting | bytes 655360
where the time goes:
time: 32.7 us; the launch traced here: 32.5 us
  Pallas kernels  29.4 us (90%)
  local copies, waits for them, and re-layouts  3.08 us (9%)
    pallas_call x1, Pallas kernels, per_device_whole_lines(): pl.pallas_call(functools.partial(step_kernel, azis, walls), out_shape=jax...  29.4 us
    unnamed x2, local copies, waits for them, and re-layouts  3.08 us

commit v1 on v0

--- a/solution.py
+++ b/solution.py
@@ -344,7 +344,7 @@
 
 
 def cycle_inverse(speeds_ref, visc, span, inverse_ref):
-    azis, variables, part = speeds_ref.shape
+    azis, part, variables = speeds_ref.shape
     cells = azis * part
     lanes = inverse_ref.shape[-1]
     lane = lax.broadcasted_iota(jnp.int32, (variables, lanes), 1)
@@ -352,9 +352,11 @@
     zero = jnp.zeros((variables, lanes), jnp.float32)
     one = jnp.ones((variables, lanes), jnp.float32)
 
+    speeds = [speeds_ref[a].T for a in range(azis)]
+
     def row(j):
         speed = jnp.broadcast_to(
-            speeds_ref[j // part][:, j % part : j % part + 1], (variables, lanes)
+            speeds[j // part][:, j % part : j % part + 1], (variables, lanes)
         )
         return band(speed, visc) + (jnp.where(own_cell == j, 1.0, 0.0),)
 
@@ -416,16 +418,16 @@
 def step_kernel(
     azis,
     walls,
-    state_ref,
-    speed_azi_ref,
-    speed_wall_ref,
-    flux_azi_ref,
-    flux_wall_ref,
-    to_wall_ref,
-    mix_char_ref,
-    from_azi_ref,
-    visc_azi_ref,
-    visc_wall_ref,
+    state_hbm,
+    speed_azi_hbm,
+    speed_wall_hbm,
+    flux_azi_hbm,
+    flux_wall_hbm,
+    to_wall_hbm,
+    mix_char_hbm,
+    from_azi_hbm,
+    visc_azi_hbm,
+    visc_wall_hbm,
     out_ref,
     send1,
     recv1,
@@ -450,8 +452,19 @@
     wall_send,
     wall_recv,
     own_sem,
+    in_sem,
+    state_ref,
+    speed_azi_ref,
+    speed_wall_ref,
+    flux_azi_ref,
+    flux_wall_ref,
+    to_wall_ref,
+    mix_char_ref,
+    from_azi_ref,
+    visc_azi_ref,
+    visc_wall_ref,
 ):
-    variables, part_j, part_k, span_all = state_ref.shape
+    variables, part_j, part_k, span_all = state_hbm.shape
     count = azis * walls
     span = span_all // count
     lanes = part_j * part_k
@@ -474,11 +487,32 @@
 
     lax.fori_loop(1, count, greet, 0)
 
+    whole = (
+        (state_hbm, state_ref),
+        (speed_azi_hbm, speed_azi_ref),
+        (speed_wall_hbm, speed_wall_ref),
+        (flux_azi_hbm, flux_azi_ref),
+        (flux_wall_hbm, flux_wall_ref),
+        (to_wall_hbm, to_wall_ref),
+        (mix_char_hbm, mix_char_ref),
+        (from_azi_hbm, from_azi_ref),
+        (visc_azi_hbm, visc_azi_ref),
+        (visc_wall_hbm, visc_wall_ref),
+    )
+    taken = [
+        pltpu.make_async_copy(there, here, in_sem.at[i]) for i, (there, here) in enumerate(whole)
+    ]
+    for copy in taken:
+        copy.start()
+    taken[0].wait()
+
     for c in range(variables):
         turned = state_ref[c].reshape(lanes, span_all).T
         for t in range(count):
-            send1[c, t] = turned[t * span : (t + 1) * span]
-
+            send1[t, c] = turned[t * span : (t + 1) * span]
+
+    for copy in taken[1:]:
+        copy.wait()
     pl.semaphore_wait(barrier, count - 1)
 
     def azi_copy(turn):
@@ -506,8 +540,8 @@
     def out_copy(turn):
         target, azi, wall = other(turn)
         return pltpu.make_async_remote_copy(
-            src_ref=send1.at[:, target],
-            dst_ref=recv1.at[me_wall, :, me_azi],
+            src_ref=send1.at[target],
+            dst_ref=recv1.at[me],
             send_sem=send1_sem.at[turn],
             recv_sem=recv1_sem.at[me],
             device_id=(azi, wall),
@@ -517,8 +551,8 @@
     def back_copy(turn):
         target, azi, wall = other(turn)
         return pltpu.make_async_remote_copy(
-            src_ref=send2.at[wall, :, azi],
-            dst_ref=recv2.at[:, me],
+            src_ref=send2.at[target],
+            dst_ref=recv2.at[me],
             send_sem=send2_sem.at[turn],
             recv_sem=recv2_sem.at[me],
             device_id=(azi, wall),
@@ -542,7 +576,7 @@
     start_all(wall_copy, walls)
     start_all(azi_copy, azis)
     start_all(out_copy, count)
-    own = pltpu.make_async_copy(send1.at[:, me], recv1.at[me_wall, :, me_azi], own_sem.at[0])
+    own = pltpu.make_async_copy(send1.at[me], recv1.at[me], own_sem.at[0])
     own.start()
     own_azi = pltpu.make_async_copy(speed_azi_ref, all_azi.at[me_azi], own_sem.at[1])
     own_azi.start()
@@ -573,15 +607,13 @@
     cycle_inverse(all_azi, viscosity(visc_azi_ref), span, cycle_inv)
 
     own.wait()
-    arrived(
-        lambda s: recv1.at[lax.rem(s, walls), :, s // walls], recv1_sem, me, count
-    )
+    arrived(lambda s: recv1.at[s], recv1_sem, me, count)
     lane = lax.broadcasted_iota(jnp.int32, (group, lanes), 1)
     piece = lane // part_k
     for c in range(variables):
         for w in range(walls):
             for a in range(azis):
-                rows_ref[c, w, pl.ds(a * span, span), :] = recv1[w, c, a]
+                rows_ref[c, w, pl.ds(a * span, span), :] = recv1[a * walls + w, c]
     for c in range(variables):
         parts = [rows_ref[c, w] for w in range(walls)]
         for m in range(part_j):
@@ -660,21 +692,27 @@
                     moved = pltpu.roll(moved, ((m - w) * part_k) % lanes, 1)
                 value = jnp.where(piece == m, moved, value) if m else moved
             for a in range(azis):
-                send2[w, c, a] = value[a * span : (a + 1) * span]
+                send2[a * walls + w, c] = value[a * span : (a + 1) * span]
 
     start_all(back_copy, count)
-    own_back = pltpu.make_async_copy(send2.at[me_wall, :, me_azi], recv2.at[:, me], own_sem.at[0])
+    own_back = pltpu.make_async_copy(send2.at[me], recv2.at[me], own_sem.at[0])
     own_back.start()
     sent_all(wall_copy, walls)
     sent_all(azi_copy, azis)
     sent_all(out_copy, count)
     own_back.wait()
-    arrived(lambda s: recv2.at[:, s], recv2_sem, me, count)
+    arrived(lambda s: recv2.at[s], recv2_sem, me, count)
     for c in range(variables):
         for s in range(count):
-            fields[c, pl.ds(s * span, span), :] = recv2[c, s]
+            fields[c, pl.ds(s * span, span), :] = recv2[s, c]
+    given = []
     for c in range(variables):
-        out_ref[c] = fields[c].T.reshape(part_j, part_k, span_all)
+        state_ref[c] = fields[c].T.reshape(part_j, part_k, span_all)
+        copy = pltpu.make_async_copy(state_ref.at[c], out_ref.at[c], in_sem.at[c])
+        copy.start()
+        given.append(copy)
+    for copy in given:
+        copy.wait()
     sent_all(back_copy, count)
 
 
@@ -696,21 +734,19 @@
     span = span_all // count
     lanes = part_j * part_k
     wall_cells = walls * part_k
-    vmem = pl.BlockSpec(memory_space=pltpu.VMEM)
-    smem = pl.BlockSpec(memory_space=pltpu.SMEM)
     f32 = jnp.float32
     dma = pltpu.SemaphoreType.DMA
     return pl.pallas_call(
         functools.partial(step_kernel, azis, walls),
         out_shape=jax.ShapeDtypeStruct(state.shape, f32),
-        in_specs=[vmem] * 3 + [smem] * 7,
-        out_specs=vmem,
+        in_specs=[pl.BlockSpec(memory_space=pl.ANY)] * 10,
+        out_specs=pl.BlockSpec(memory_space=pl.ANY),
         scratch_shapes=[
-            pltpu.VMEM((variables, count, span, lanes), f32),
-            pltpu.VMEM((walls, variables, azis, span, lanes), f32),
-            pltpu.VMEM((walls, variables, azis, span, lanes), f32),
-            pltpu.VMEM((variables, count, span, lanes), f32),
-            pltpu.VMEM((azis,) + speed_azi.shape, f32),
+            pltpu.VMEM((count, variables, span, lanes), f32),
+            pltpu.VMEM((count, variables, span, lanes), f32),
+            pltpu.VMEM((count, variables, span, lanes), f32),
+            pltpu.VMEM((count, variables, span, lanes), f32),
+            pltpu.VMEM((azis,) + speed_azi.shape[::-1], f32),
             pltpu.VMEM((walls,) + speed_wall.shape, f32),
             pltpu.VMEM((wall_cells, variables, lanes), f32),
             pltpu.VMEM((wall_cells, variables, lanes), f32),
@@ -729,11 +765,22 @@
             dma((walls,)),
             dma((walls,)),
             dma((3,)),
+            dma((10,)),
+            pltpu.VMEM(state.shape, f32),
+            pltpu.VMEM(speed_azi.shape[::-1], f32),
+            pltpu.VMEM(speed_wall.shape, f32),
+            pltpu.SMEM(flux_azi.shape, f32),
+            pltpu.SMEM(flux_wall.shape, f32),
+            pltpu.SMEM(to_wall.shape, f32),
+            pltpu.SMEM(mix_char.shape, f32),
+            pltpu.SMEM(from_azi.shape, f32),
+            pltpu.SMEM(visc_azi.shape, f32),
+            pltpu.SMEM(visc_wall.shape, f32),
         ],
         compiler_params=pltpu.CompilerParams(collective_id=0, has_side_effects=True),
     )(
         state,
-        speed_azi,
+        speed_azi.T,
         speed_wall,
         flux_azi,
         flux_wall,

time: 32.7 us -> 30 us (0.917)
  local copies, waits for them, and re-layouts: 3.08 us -> 1.72 us
  Pallas kernels: 29.4 us -> 28.1 us
    unnamed x2 -> x1, local copies, waits for them, and re-layouts: 3.08 us -> 1.72 us
    pallas_call x1, Pallas kernels: 29.4 us -> 28.1 us  [per_device_whole_lines(): pl.pallas_call(functools.partial(step_kernel, azis, walls), out_shape=jax...]
where the time goes in v1:
time: 30 us; the launch traced here: 29.8 us
  Pallas kernels  28.1 us (94%)
  local copies, waits for them, and re-layouts  1.72 us (6%)
    pallas_call x1, Pallas kernels, per_device_whole_lines(): pl.pallas_call(functools.partial(step_kernel, azis, walls), out_shape=jax...  28.1 us
    unnamed x1, local copies, waits for them, and re-layouts  1.72 us

profile of v1, /device:TPU:25, one launch (start us, length us, event | category | flops | bytes accessed | tf_op | source)
XLA Modules:
  0.0 29.8 jit_solution(6437420821003895481)
XLA Ops:
  0.0 28.1 %shard_map.100 = f32[5,4,32,128]{3,2,1,0:T(8,128)} custom-call(f32[5,4,32,128]{3,2,1,0:T(8,128)} %state_hbm.1, f32[4,5]{1,0:T(4,128)} %bitcast.1, f32[5,32]{1,0:T(8,128)} %speed_wall_hbm.1, f32[5,5]{1,0:T(8,128)} %flux_azi_hbm.1, f32[5,5]{1,0:T(8,128)} %flux_wall_hbm.1, f32[5,5]{1,0:T(8,128)} %to_wall_hbm.1, f32[5,5]{1,0:T(8,128)} %mix_char_hbm.1, ...), custom_call_target="tpu_custom_call" | custom-call | tf_op jit(solution)/shard_map/pallas_call | solution.py:739
  28.1 1.7 %copy.12 = f32[5,4,32,128]{3,2,1,0:T(8,128)} copy(f32[5,4,32,128]{3,2,1,0:T(8,128)} %shard_map.100) | data formatting | bytes 655360
